TPU v7x, 32 devices: a whole 2x2x4 slice. The times are simulated.
32 devices in a mesh: row: 8 (over z, core), col: 4 (over y, x).
Axes of the slice: x: 2, y: 2, z: 4, core: 2. Of those that a mesh axis runs over, the one named last changes fastest.
Arguments:
- affinity: float32 [16384, 16384], P('row', 'col'), as said below
Outputs:
- reduced: float32 [16384, 16384], P('row', 'col')
Inputs may be any that keep to these rules, and one draw needn't show every extreme that they name: The matrix that affinity stores is exactly symmetric in global indexing.
All inputs are finite; a program needn't handle non-finite values.
Results may differ from a plain program's by a relative error of at most 0.0003.
Values sent between devices are 32-bit elements; how exact they have to be, the bound alone decides.
No kernel may reach another device: no remote copies, remote signals or barrier semaphores. Data moves between devices by JAX's collectives and lax.ppermute only.
A program may use at most 192 MiB of HBM per device.

v0:
```python
import jax
import jax.numpy as jnp
from jax import lax
from jax.sharding import PartitionSpec as P

B = 256
PANELS = 2
NS_STEPS = 12
PRECISE = lax.Precision.HIGHEST


def spread(block, axis, owner):
    block = jnp.where(lax.axis_index(axis) == owner, block, jnp.zeros_like(block))
    return lax.psum(block, axis)


def matmul(first_op, second_op, first_dim, second_dim):
    return lax.dot_general(
        first_op,
        second_op,
        (((first_dim,), (second_dim,)), ((), ())),
        precision=PRECISE,
        preferred_element_type=jnp.float32,
    )


def lower_inverse(square):
    lower_factor = jnp.linalg.cholesky(square)
    identity = jnp.eye(square.shape[0], dtype=jnp.float32)
    return lax.linalg.triangular_solve(lower_factor, identity, left_side=True, lower=True)


def reflector_parts(gram_matrix, top_block):
    inverse_low = lower_inverse(gram_matrix)
    top_basis = matmul(top_block, inverse_low, 1, 1)
    polar_part = top_basis
    for repeat in range(NS_STEPS):
        polar_part = 1.5 * polar_part - 0.5 * matmul(
            polar_part, matmul(polar_part, polar_part, 0, 0), 1, 0
        )
    cross_term = matmul(polar_part, top_basis, 0, 0)
    identity = jnp.eye(gram_matrix.shape[0], dtype=jnp.float32)
    metric = identity + cross_term + cross_term.T + matmul(polar_part, polar_part, 0, 0)
    metric_inv = lower_inverse(metric)
    middle = 2.0 * matmul(metric_inv, metric_inv, 0, 0)
    return (inverse_low, polar_part, middle)


def body(affinity):
    rows_here = affinity.shape[0]
    cols_here = affinity.shape[1]
    row_count = lax.axis_size("row")
    col_count = lax.axis_size("col")
    row_rank = lax.axis_index("row")
    col_rank = lax.axis_index("col")
    fold_count = row_count // col_count
    row_blocks = jnp.arange(rows_here, dtype=jnp.int32) // B * row_count + row_rank
    matrix = affinity

    def to_columns(row_panel):
        pieces = []
        for part_num in range(fold_count):
            pieces.append(spread(row_panel, "row", col_rank + part_num * col_count))
        stacked = jnp.stack(pieces).reshape(fold_count, rows_here // B, B, B)
        return jnp.transpose(stacked, (3, 1, 0, 2)).reshape(B, cols_here)

    for panel_num in range(PANELS):
        col_start = panel_num // col_count * B
        owned_cols = matrix[:, col_start : col_start + B]
        panel_rows = spread(owned_cols, "col", panel_num % col_count)
        panel_rows = jnp.where((row_blocks > panel_num)[:, None], panel_rows, 0.0)
        top_start = (panel_num + 1) // row_count * B
        top_mask = (row_rank == (panel_num + 1) % row_count).astype(jnp.float32)
        top_piece = top_mask * panel_rows[top_start : top_start + B]
        gram_matrix, top_block = lax.psum((matmul(panel_rows, panel_rows, 0, 0), top_piece), "row")
        inverse_low, polar_part, middle = reflector_parts(gram_matrix, top_block)
        reflect_rows = (
            matmul(panel_rows, inverse_low, 1, 1)
            .at[top_start : top_start + B]
            .add(top_mask * polar_part)
        )
        reflect_cols = to_columns(reflect_rows)
        local_product = matmul(matrix, reflect_cols, 1, 1)
        product_rows = lax.psum(local_product, "col")
        image_rows = matmul(product_rows, middle, 1, 0)
        coupling = lax.psum(matmul(reflect_rows, image_rows, 0, 0), "row")
        shift_term = matmul(middle, coupling, 1, 0)
        companion_rows = image_rows - 0.5 * matmul(reflect_rows, shift_term, 1, 0)
        companion_cols = to_columns(companion_rows)
        matrix = matrix - matmul(
            jnp.concatenate((reflect_rows, companion_rows), 1),
            jnp.concatenate((companion_cols, reflect_cols), 0),
            1,
            0,
        )
    return matrix


def solution(mesh):
    return jax.shard_map(
        body, mesh=mesh, in_specs=(P("row", "col"),), out_specs=P("row", "col"), check_vma=False
    )
```

profile of v0, /device:TPU:0, one launch (start us, length us, event | category | flops | bytes accessed | tf_op | source)
XLA Modules:
  0.0 1348.9 jit_solution(7293248256234329230)
XLA Ops:
  6.5 3.0 slice_select_fusion.1
  9.7 73.0 %all-reduce.20.cloned.1.call-done = f32[2048,256]{1,0:T(8,128)} async-done(((f32[2048,256]{1,0:T(8,128)}), f32[2048,256]{1,0:T(8,128)}) %all-reduce.20.cloned.1.call-update) | async-done | bytes 2097168 | tf_op jit(solution)/shard_map/psum | solution.py:14
  84.6 4.3 fusion.102
  89.9 56.5 %all-reduce.42.cloned.1.call-done = (f32[256,256]{0,1:T(8,128)}, f32[256,256]{1,0:T(8,128)}) async-done(((f32[256,256]{0,1:T(8,128)}, f32[256,256]{1,0:T(8,128)}), (f32[256,256]{0,1:T(8,128)}, f32[256,256]{1,0:T(8,128)})) %all-reduce.42.cloned.1.call-update) | async-done | bytes 524304 | tf_op jit(solution)/shard_map/psum | solution.py:75
  148.5 11.7 cholesky.214
  160.3 9.8 custom-call.17
  170.6 11.7 cholesky.231
  184.4 4.1 while.10
  188.5 19.9 %custom-call.18 = f32[2,128,128]{1,2,0:T(8,128)S(1)} custom-call(f32[2,128,128]{2,1,0:T(8,128)S(1)} %get-tuple-element.57), custom_call_target="InvertDiagBlocksLowerTriangular" | custom-call | tf_op jit(solution)/shard_map/triangular_solve/custom-call.0 | solution.py:30
  209.4 3.5 fusion.54
  229.7 11.7 cholesky.248
  241.5 9.8 custom-call.19
  251.8 72.1 %all-reduce.40.cloned.1.call-done = (f32[1,8,256,256]{3,2,0,1:T(8,128)}, f32[1,8,256,256]{3,2,0,1:T(8,128)}) async-done(((f32[1,8,256,256]{3,2,0,1:T(8,128)}, f32[1,8,256,256]{3,2,0,1:T(8,128)}), (f32[1,8,256,256]{3,2,0,1:T(8,128)}, f32[1,8,256,256]{3,2,0,1:T(8,128)})) %all-reduce.40.cloned.1.call-update) | async-done | bytes 4194320 | tf_op jit(solution)/shard_map/psum | solution.py:14
  328.6 58.3 %convolution_bitcast_fusion = f32[2048,256]{0,1:T(8,128)} fusion(f32[256,4096]{0,1:T(8,128)S(1)} %bitcast.302, f32[2048,4096]{1,0:T(8,128)} %param.8), kind=kOutput, calls=%fused_computation.30 | convolution fusion | flops 25769803776 | bytes 39845888 | tf_op jit(solution)/shard_map/dot_general | solution.py:18
  387.7 11.7 cholesky.265
  401.4 3.9 while.11
  405.3 19.7 %custom-call.20 = f32[2,128,128]{1,2,0:T(8,128)S(1)} custom-call(f32[2,128,128]{2,1,0:T(8,128)S(1)} %get-tuple-element.58), custom_call_target="InvertDiagBlocksLowerTriangular" | custom-call | tf_op jit(solution)/shard_map/triangular_solve/custom-call.0 | solution.py:30
  426.6 30.3 %all-reduce.22.cloned.1.call-done = f32[2048,256]{0,1:T(8,128)} async-done(((f32[2048,256]{0,1:T(8,128)}), f32[2048,256]{0,1:T(8,128)}) %all-reduce.22.cloned.1.call-update) | async-done | bytes 2097168 | tf_op jit(solution)/shard_map/psum | solution.py:84
  456.9 5.2 fusion.116
  463.4 4.2 fusion.117
  467.9 55.3 %all-reduce.24.cloned.1.call-done = f32[256,256]{1,0:T(8,128)} async-done(((f32[256,256]{1,0:T(8,128)}), f32[256,256]{1,0:T(8,128)}) %all-reduce.24.cloned.1.call-update) | async-done | bytes 262160 | tf_op jit(solution)/shard_map/psum | solution.py:86
  524.6 6.0 broadcast_select_fusion.6
  530.7 95.7 %all-reduce.38.cloned.1.call-done = (f32[1,8,256,256]{3,2,0,1:T(8,128)}, f32[1,8,256,256]{3,2,0,1:T(8,128)}) async-done(((f32[1,8,256,256]{3,2,0,1:T(8,128)}, f32[1,8,256,256]{3,2,0,1:T(8,128)}), (f32[1,8,256,256]{3,2,0,1:T(8,128)}, f32[1,8,256,256]{3,2,0,1:T(8,128)})) %all-reduce.38.cloned.1.call-update) | async-done | bytes 4194320 | tf_op jit(solution)/shard_map/psum | solution.py:14
  630.5 59.6 %convolution_subtract_fusion.1 = f32[2048,4096]{1,0:T(8,128)} fusion(f32[2048,4096]{1,0:T(8,128)} %param.8, f32[256,4096]{0,1:T(8,128)S(1)} %bitcast.303, f32[256,4096]{0,1:T(8,128)S(1)} %bitcast.307, f32[2048,256]{1,0:T(8,128)S(1)} %copy-done.8, f32[2048,256]{1,0:T(8,128)S(1)} %get-tuple-element.139), kind=kOutput, calls=%fused_computation.9 | convolution fusion | flops 51551141888 | bytes 79691776 | tf_op jit(solution)/shard_map/dot_general | solution.py:18
  690.0 3.0 slice_select_fusion
  693.1 69.6 %all-reduce.26.cloned.1.call-done = f32[2048,256]{1,0:T(8,128)} async-done(((f32[2048,256]{1,0:T(8,128)}), f32[2048,256]{1,0:T(8,128)}) %all-reduce.26.cloned.1.call-update) | async-done | bytes 2097168 | tf_op jit(solution)/shard_map/psum | solution.py:14
  764.7 4.3 fusion.119
  770.2 56.3 %all-reduce.36.cloned.1.call-done = (f32[256,256]{0,1:T(8,128)}, f32[256,256]{1,0:T(8,128)}) async-done(((f32[256,256]{0,1:T(8,128)}, f32[256,256]{1,0:T(8,128)}), (f32[256,256]{0,1:T(8,128)}, f32[256,256]{1,0:T(8,128)})) %all-reduce.36.cloned.1.call-update) | async-done | bytes 524304 | tf_op jit(solution)/shard_map/psum | solution.py:75
  828.6 11.7 cholesky.282
  841.1 9.8 custom-call.21
  851.4 11.7 cholesky.299
  865.1 4.0 while.12
  869.1 19.8 %custom-call.22 = f32[2,128,128]{1,2,0:T(8,128)S(1)} custom-call(f32[2,128,128]{2,1,0:T(8,128)S(1)} %get-tuple-element.59), custom_call_target="InvertDiagBlocksLowerTriangular" | custom-call | tf_op jit(solution)/shard_map/triangular_solve/custom-call.0 | solution.py:30
  890.0 3.5 fusion.52
  910.0 11.7 cholesky.316
  921.8 9.8 custom-call.23
  932.1 72.1 %all-reduce.34.cloned.1.call-done = (f32[1,8,256,256]{3,2,0,1:T(8,128)}, f32[1,8,256,256]{3,2,0,1:T(8,128)}) async-done(((f32[1,8,256,256]{3,2,0,1:T(8,128)}, f32[1,8,256,256]{3,2,0,1:T(8,128)}), (f32[1,8,256,256]{3,2,0,1:T(8,128)}, f32[1,8,256,256]{3,2,0,1:T(8,128)})) %all-reduce.34.cloned.1.call-update) | async-done | bytes 4194320 | tf_op jit(solution)/shard_map/psum | solution.py:14
  1008.9 31.4 %fusion.132 = f32[2048,256]{1,0:T(8,128)} fusion(f32[2048,4096]{1,0:T(8,128)} %convolution_subtract_fusion.1, f32[256,4096]{0,1:T(8,128)S(1)} %bitcast.304), kind=kOutput, calls=%fused_computation.258 | convolution fusion | flops 25769803776 | bytes 39845888 | tf_op jit(solution)/shard_map/dot_general | solution.py:18
  1041.0 11.7 cholesky.333
  1054.7 4.0 while.13
  1058.7 19.7 %custom-call.24 = f32[2,128,128]{1,2,0:T(8,128)S(1)} custom-call(f32[2,128,128]{2,1,0:T(8,128)S(1)} %get-tuple-element.60), custom_call_target="InvertDiagBlocksLowerTriangular" | custom-call | tf_op jit(solution)/shard_map/triangular_solve/custom-call.0 | solution.py:30
  1080.0 30.1 %all-reduce.28.cloned.1.call-done = f32[2048,256]{1,0:T(8,128)} async-done(((f32[2048,256]{1,0:T(8,128)}), f32[2048,256]{1,0:T(8,128)}) %all-reduce.28.cloned.1.call-update) | async-done | bytes 2097168 | tf_op jit(solution)/shard_map/psum | solution.py:84
  1110.2 3.5 fusion.134
  1115.0 4.2 fusion.135
  1119.3 55.5 %all-reduce.30.cloned.1.call-done = f32[256,256]{1,0:T(8,128)} async-done(((f32[256,256]{1,0:T(8,128)}), f32[256,256]{1,0:T(8,128)}) %all-reduce.30.cloned.1.call-update) | async-done | bytes 262160 | tf_op jit(solution)/shard_map/psum | solution.py:86
  1176.1 6.1 broadcast_select_fusion.1
  1182.2 95.7 %all-reduce.32.cloned.1.call-done = (f32[1,8,256,256]{3,2,0,1:T(8,128)}, f32[1,8,256,256]{3,2,0,1:T(8,128)}) async-done(((f32[1,8,256,256]{3,2,0,1:T(8,128)}, f32[1,8,256,256]{3,2,0,1:T(8,128)}), (f32[1,8,256,256]{3,2,0,1:T(8,128)}, f32[1,8,256,256]{3,2,0,1:T(8,128)})) %all-reduce.32.cloned.1.call-update) | async-done | bytes 4194320 | tf_op jit(solution)/shard_map/psum | solution.py:14
  1282.1 59.7 %convolution_subtract_fusion = f32[2048,4096]{1,0:T(8,128)} fusion(f32[2048,4096]{1,0:T(8,128)} %convolution_subtract_fusion.1, f32[256,4096]{0,1:T(8,128)S(1)} %bitcast.305, f32[256,4096]{0,1:T(8,128)S(1)} %bitcast.306, f32[2048,256]{1,0:T(8,128)S(1)} %copy-done.9, f32[2048,256]{1,0:T(8,128)S(1)} %get-tuple-element.146), kind=kOutput, calls=%fused_computation.8 | convolution fusion | flops 51551141888 | bytes 79691776 | tf_op jit(solution)/shard_map/dot_general | solution.py:18
  (206 shorter events, 94.4 us)
Async XLA Ops:
  6.5 76.1 %all-reduce.20.cloned.1.call-start = ((), (), s32[]{:S(2)}) async-start(), calls=%async_computation | async-start | bytes 4194304 | tf_op jit(solution)/shard_map/psum | solution.py:14
  9.6 136.8 %all-reduce.42.cloned.1.call-start = ((), (), s32[]{:S(2)}) async-start(), calls=%async_computation.11 | async-start | bytes 1048576 | tf_op jit(solution)/shard_map/psum | solution.py:75
  84.6 4.3 copy-start.4
  89.6 234.3 %all-reduce.40.cloned.1.call-start = ((), (), s32[]{:S(2)}) async-start(), calls=%async_computation.10 | async-start | bytes 8388608 | tf_op jit(solution)/shard_map/psum | solution.py:14
  209.4 3.5 copy-start.10
  228.1 228.8 %all-reduce.22.cloned.1.call-start = ((), (), s32[]{:S(2)}) async-start(), calls=%async_computation.1 | async-start | bytes 4194304 | tf_op jit(solution)/shard_map/psum | solution.py:84
  326.6 2.0 copy-start
  387.0 136.2 %all-reduce.24.cloned.1.call-start = ((), (), s32[]{:S(2)}) async-start(), calls=%async_computation.2 | async-start | bytes 524288 | tf_op jit(solution)/shard_map/psum | solution.py:86
  462.1 1.3 copy-start.7
  467.6 158.7 %all-reduce.38.cloned.1.call-start = ((), (), s32[]{:S(2)}) async-start(), calls=%async_computation.9 | async-start | bytes 8388608 | tf_op jit(solution)/shard_map/psum | solution.py:14
  530.6 232.1 %all-reduce.26.cloned.1.call-start = ((), (), s32[]{:S(2)}) async-start(), calls=%async_computation.3 | async-start | bytes 4194304 | tf_op jit(solution)/shard_map/psum | solution.py:14
  626.3 3.4 copy-start.1
  626.3 4.1 copy-start.8
  693.1 133.5 %all-reduce.36.cloned.1.call-start = ((), (), s32[]{:S(2)}) async-start(), calls=%async_computation.8 | async-start | bytes 1048576 | tf_op jit(solution)/shard_map/psum | solution.py:75
  764.7 4.3 copy-start.5
  769.8 234.5 %all-reduce.34.cloned.1.call-start = ((), (), s32[]{:S(2)}) async-start(), calls=%async_computation.7 | async-start | bytes 8388608 | tf_op jit(solution)/shard_map/psum | solution.py:14
  890.0 3.5 copy-start.11
  908.4 201.7 %all-reduce.28.cloned.1.call-start = ((), (), s32[]{:S(2)}) async-start(), calls=%async_computation.4 | async-start | bytes 4194304 | tf_op jit(solution)/shard_map/psum | solution.py:84
  1006.9 1.9 copy-start.2
  1040.3 134.5 %all-reduce.30.cloned.1.call-start = ((), (), s32[]{:S(2)}) async-start(), calls=%async_computation.5 | async-start | bytes 524288 | tf_op jit(solution)/shard_map/psum | solution.py:86
  1113.7 1.3 copy-start.6
  1119.2 158.7 %all-reduce.32.cloned.1.call-start = ((), (), s32[]{:S(2)}) async-start(), calls=%async_computation.6 | async-start | bytes 8388608 | tf_op jit(solution)/shard_map/psum | solution.py:14
  1278.0 3.4 copy-start.3
  1278.0 4.1 copy-start.9
Sparse Core Ops, SparseCore 0:
  10.4 72.1 all-reduce.19
  89.8 56.6 all-reduce.41
  228.2 95.6 all-reduce.39
  387.1 69.7 all-reduce.21
  467.8 55.4 all-reduce.23
  530.7 95.5 all-reduce.37
  693.2 69.4 all-reduce.25
  769.9 56.6 all-reduce.35
  908.6 95.6 all-reduce.33
  1040.4 69.6 all-reduce.27
  1119.4 55.4 all-reduce.29
  1182.4 95.5 all-reduce.31
where the time goes:
time: 1350 us
  waiting for transfers between devices  763 us (57%)
  matrix products  291 us (22%)
  other arithmetic  246 us (18%)
  local copies, waits for them, and re-layouts  27.7 us (2%)
  between operations  19.9 us (1%)
    psum x6, waiting for transfers between devices, spread(): return lax.psum(block, axis)  478 us
    dot_general x72, matrix products, matmul(): lax.dot_general(first_op, second_op, (((first_dim,), (second_dim,)), ((),...  285 us
    another operation x27, other arithmetic, lower_inverse(): lower_factor = jnp.linalg.cholesky(square)  138 us
    psum x2, waiting for transfers between devices, body(): lax.psum((matmul(panel_rows, panel_rows, 0, 0), top_piece), 'row')  113 us
    psum x2, waiting for transfers between devices, body(): coupling = lax.psum(matmul(reflect_rows, image_rows, 0, 0), 'row')  111 us
    another operation x9, other arithmetic, lower_inverse(): lax.linalg.triangular_solve(lower_factor, identity, left_side=True, lower...  79.2 us
    psum x2, waiting for transfers between devices, body(): product_rows = lax.psum(local_product, 'col')  60.4 us
  transfers between devices with their start and end apart: 12, of which 12 were waited for; matrix products, arithmetic and copies ran while one was open for 9% of the time, Pallas kernels for 0%

commit v1 on v0

--- a/solution.py
+++ b/solution.py
@@ -11,7 +11,7 @@
 
 def spread(block, axis, owner):
     block = jnp.where(lax.axis_index(axis) == owner, block, jnp.zeros_like(block))
-    return lax.psum(block, axis)
+    return jnp.sum(lax.all_gather(block, axis), axis=0)
 
 
 def matmul(first_op, second_op, first_dim, second_dim):

time: 1350 us -> 2440 us (1.81)
  waiting for transfers between devices: 763 us -> 1510 us
  local copies, waits for them, and re-layouts: 27.7 us -> 282 us
  other arithmetic: 246 us -> 308 us
    all_gather x0 -> x10, waiting for transfers between devices: none -> 1200 us  [spread(): return jnp.sum(lax.all_gather(block, axis), axis=0)]
    psum x6 -> x0, waiting for transfers between devices: 478 us -> none  [spread(): return lax.psum(block, axis)]
    unnamed x24 -> x33, local copies, waits for them, and re-layouts: 9.23 us -> 189 us
    reduce_sum x0 -> x10, other arithmetic: none -> 65.9 us  [spread(): return jnp.sum(lax.all_gather(block, axis), axis=0)]
    sub x0 -> x1, local copies, waits for them, and re-layouts: none -> 31.1 us  [body(): matrix - matmul(jnp.concatenate((reflect_rows, companion_rows), 1), jnp.c...]
  transfers between devices with their start and end apart: 12 -> 16, of which waited for: 12 -> 16; matrix products, arithmetic and copies ran while one was open for 9% -> 9% of each run, Pallas kernels for 0% -> 0%
where the time goes in v1:
time: 2440 us; the launch traced here: 2430 us
  waiting for transfers between devices  1510 us (62%)
  matrix products  313 us (13%)
  other arithmetic  308 us (13%)
  local copies, waits for them, and re-layouts  282 us (12%)
    all_gather x10, waiting for transfers between devices, spread(): return jnp.sum(lax.all_gather(block, axis), axis=0)  1200 us
    dot_general x72, matrix products, matmul(): lax.dot_general(first_op, second_op, (((first_dim,), (second_dim,)), ((),...  307 us
    unnamed x33, local copies, waits for them, and re-layouts  189 us
    another operation x27, other arithmetic, lower_inverse(): lower_factor = jnp.linalg.cholesky(square)  138 us
    psum x2, waiting for transfers between devices, body(): lax.psum((matmul(panel_rows, panel_rows, 0, 0), top_piece), 'row')  113 us
    psum x2, waiting for transfers between devices, body(): coupling = lax.psum(matmul(reflect_rows, image_rows, 0, 0), 'row')  111 us
    psum x2, waiting for transfers between devices, body(): product_rows = lax.psum(local_product, 'col')  80.4 us
    another operation x9, other arithmetic, lower_inverse(): lax.linalg.triangular_solve(lower_factor, identity, left_side=True, lower...  79.4 us
  transfers between devices with their start and end apart: 16, of which 16 were waited for; matrix products, arithmetic and copies ran while one was open for 9% of the time, Pallas kernels for 0%

profile of v1, /device:TPU:0, one launch (start us, length us, event | category | flops | bytes accessed | tf_op | source)
XLA Modules:
  0.0 2433.1 jit_solution(1746692952090603767)
XLA Ops:
  6.5 33.3 %copy.43 = f32[2048,4096]{0,1:T(8,128)} copy(f32[2048,4096]{1,0:T(8,128)} %param.8) | data formatting | bytes 67108864 | tf_op args[0]
  43.2 90.3 %all-gather.21.cloned.1.call-done = f32[8192,256]{0,1:T(8,128)} async-done(((f32[2048,256]{0,1:T(8,128)}), f32[8192,256]{0,1:T(8,128)}) %all-gather.21.cloned.1.call-update) | async-done | bytes 8388624 | tf_op jit(solution)/shard_map/all_gather | solution.py:14
  133.5 10.8 reshape.155
  157.0 56.2 %all-reduce.20.cloned.1.call-done = (f32[256,256]{0,1:T(8,128)}, f32[256,256]{0,1:T(8,128)}) async-done(((f32[256,256]{0,1:T(8,128)}, f32[256,256]{0,1:T(8,128)}), (f32[256,256]{0,1:T(8,128)}, f32[256,256]{0,1:T(8,128)})) %all-reduce.20.cloned.1.call-update) | async-done | bytes 524304 | tf_op jit(solution)/shard_map/psum | solution.py:75
  215.3 11.7 cholesky.214
  227.1 9.8 custom-call.17
  237.4 11.7 cholesky.231
  254.9 19.9 custom-call.18
  297.0 11.7 cholesky.248
  308.8 9.8 custom-call.19
  319.1 11.7 cholesky.265
  330.8 114.8 %all-gather.23.cloned.1.call-done = f32[16384,256]{0,1:T(8,128)} async-done(((f32[2048,256]{0,1:T(8,128)}), f32[16384,256]{0,1:T(8,128)}) %all-gather.23.cloned.1.call-update) | async-done | bytes 16777232 | tf_op jit(solution)/shard_map/all_gather | solution.py:14
  445.5 17.7 copy.71
  472.9 123.4 %all-gather.25.cloned.1.call-done = f32[16384,256]{0,1:T(8,128)} async-done(((f32[2048,256]{0,1:T(8,128)}), f32[16384,256]{0,1:T(8,128)}) %all-gather.25.cloned.1.call-update) | async-done | bytes 16777232 | tf_op jit(solution)/shard_map/all_gather | solution.py:14
  596.3 17.6 copy.72
  628.2 58.4 %convolution_bitcast_fusion = f32[2048,256]{0,1:T(8,128)} fusion(f32[256,4096]{0,1:T(8,128)S(1)} %bitcast.346, f32[2048,4096]{1,0:T(8,128)} %param.8), kind=kOutput, calls=%fused_computation.38 | convolution fusion | flops 25769803776 | bytes 39845888 | tf_op jit(solution)/shard_map/dot_general | solution.py:18
  693.1 19.7 custom-call.20
  714.4 40.2 %all-reduce.10.cloned.1.call-done = f32[2048,256]{0,1:T(8,128)} async-done(((f32[2048,256]{0,1:T(8,128)}), f32[2048,256]{0,1:T(8,128)}) %all-reduce.10.cloned.1.call-update) | async-done | bytes 2097168 | tf_op jit(solution)/shard_map/psum | solution.py:84
  762.3 55.5 %all-reduce.12.cloned.1.call-done = f32[256,256]{1,0:T(8,128)} async-done(((f32[256,256]{1,0:T(8,128)}), f32[256,256]{1,0:T(8,128)}) %all-reduce.12.cloned.1.call-update) | async-done | bytes 262160 | tf_op jit(solution)/shard_map/psum | solution.py:86
  826.6 149.5 %all-gather.27.cloned.1.call-done = f32[16384,256]{0,1:T(8,128)} async-done(((f32[2048,256]{0,1:T(8,128)}), f32[16384,256]{0,1:T(8,128)}) %all-gather.27.cloned.1.call-update) | async-done | bytes 16777232 | tf_op jit(solution)/shard_map/all_gather | solution.py:14
  976.1 17.7 copy.73
  1001.4 125.6 %all-gather.29.cloned.1.call-done = f32[16384,256]{0,1:T(8,128)} async-done(((f32[2048,256]{0,1:T(8,128)}), f32[16384,256]{0,1:T(8,128)}) %all-gather.29.cloned.1.call-update) | async-done | bytes 16777232 | tf_op jit(solution)/shard_map/all_gather | solution.py:14
  1127.0 17.6 copy.75
  1159.3 61.0 %convolution_subtract_fusion.1 = f32[2048,4096]{0,1:T(8,128)} fusion(f32[2048,4096]{0,1:T(8,128)} %copy.43, f32[256,4096]{0,1:T(8,128)} %bitcast.347, f32[256,4096]{0,1:T(8,128)} %bitcast.350, f32[2048,256]{0,1:T(8,128)} %get-tuple-element.135, f32[2048,256]{0,1:T(8,128)S(1)} %get-tuple-element.131), kind=kOutput, calls=%fused_computation.17 | convolution fusion | flops 51551141888 | bytes 79691776 | tf_op jit(solution)/shard_map/dot_general | solution.py:18
  1223.6 85.7 %all-gather.31.cloned.1.call-done = f32[8192,256]{0,1:T(8,128)} async-done(((f32[2048,256]{0,1:T(8,128)}), f32[8192,256]{0,1:T(8,128)}) %all-gather.31.cloned.1.call-update) | async-done | bytes 8388624 | tf_op jit(solution)/shard_map/all_gather | solution.py:14
  1309.4 11.2 reshape.160
  1333.0 56.6 %all-reduce.18.cloned.1.call-done = (f32[256,256]{0,1:T(8,128)}, f32[256,256]{0,1:T(8,128)}) async-done(((f32[256,256]{0,1:T(8,128)}, f32[256,256]{0,1:T(8,128)}), (f32[256,256]{0,1:T(8,128)}, f32[256,256]{0,1:T(8,128)})) %all-reduce.18.cloned.1.call-update) | async-done | bytes 524304 | tf_op jit(solution)/shard_map/psum | solution.py:75
  1391.6 11.7 cholesky.282
  1403.4 9.8 custom-call.21
  1413.7 11.7 cholesky.299
  1431.8 20.1 custom-call.22
  1473.8 11.7 cholesky.316
  1485.6 9.8 custom-call.23
  1495.9 11.7 cholesky.333
  1507.6 114.8 %all-gather.33.cloned.1.call-done = f32[16384,256]{0,1:T(8,128)} async-done(((f32[2048,256]{0,1:T(8,128)}), f32[16384,256]{0,1:T(8,128)}) %all-gather.33.cloned.1.call-update) | async-done | bytes 16777232 | tf_op jit(solution)/shard_map/all_gather | solution.py:14
  1622.4 18.0 copy.77
  1650.0 123.2 %all-gather.35.cloned.1.call-done = f32[16384,256]{0,1:T(8,128)} async-done(((f32[2048,256]{0,1:T(8,128)}), f32[16384,256]{0,1:T(8,128)}) %all-gather.35.cloned.1.call-update) | async-done | bytes 16777232 | tf_op jit(solution)/shard_map/all_gather | solution.py:14
  1773.2 17.6 copy.78
  1805.1 57.1 %fusion.132 = f32[2048,256]{1,0:T(8,128)} fusion(f32[2048,4096]{0,1:T(8,128)} %convolution_subtract_fusion.1, f32[256,4096]{0,1:T(8,128)S(1)} %bitcast.348), kind=kOutput, calls=%fused_computation.266 | convolution fusion | flops 25769803776 | bytes 39845888 | tf_op jit(solution)/shard_map/dot_general | solution.py:18
  1868.6 19.7 custom-call.24
  1889.9 40.2 %all-reduce.14.cloned.1.call-done = f32[2048,256]{1,0:T(8,128)} async-done(((f32[2048,256]{1,0:T(8,128)}), f32[2048,256]{1,0:T(8,128)}) %all-reduce.14.cloned.1.call-update) | async-done | bytes 2097168 | tf_op jit(solution)/shard_map/psum | solution.py:84
  1937.7 55.5 %all-reduce.16.cloned.1.call-done = f32[256,256]{1,0:T(8,128)} async-done(((f32[256,256]{1,0:T(8,128)}), f32[256,256]{1,0:T(8,128)}) %all-reduce.16.cloned.1.call-update) | async-done | bytes 262160 | tf_op jit(solution)/shard_map/psum | solution.py:86
  2001.7 149.7 %all-gather.39.cloned.1.call-done = f32[16384,256]{0,1:T(8,128)} async-done(((f32[2048,256]{0,1:T(8,128)}), f32[16384,256]{0,1:T(8,128)}) %all-gather.39.cloned.1.call-update) | async-done | bytes 16777232 | tf_op jit(solution)/shard_map/all_gather | solution.py:14
  2151.4 18.0 copy.81
  2177.0 125.2 %all-gather.37.cloned.1.call-done = f32[16384,256]{0,1:T(8,128)} async-done(((f32[2048,256]{0,1:T(8,128)}), f32[16384,256]{0,1:T(8,128)}) %all-gather.37.cloned.1.call-update) | async-done | bytes 16777232 | tf_op jit(solution)/shard_map/all_gather | solution.py:14
  2302.2 17.6 copy.79
  2334.4 61.0 %convolution_subtract_fusion = f32[2048,4096]{0,1:T(8,128)} fusion(f32[2048,4096]{0,1:T(8,128)} %convolution_subtract_fusion.1, f32[256,4096]{0,1:T(8,128)} %bitcast.349, f32[256,4096]{0,1:T(8,128)} %bitcast.351, f32[2048,256]{0,1:T(8,128)} %get-tuple-element.142, f32[2048,256]{0,1:T(8,128)S(1)} %get-tuple-element.138), kind=kOutput, calls=%fused_computation.16 | convolution fusion | flops 51551141888 | bytes 79691776 | tf_op jit(solution)/shard_map/dot_general | solution.py:18
  2395.3 31.1 %copy.56 = f32[2048,4096]{1,0:T(8,128)} copy(f32[2048,4096]{0,1:T(8,128)} %convolution_subtract_fusion) | data formatting | bytes 67108864 | tf_op jit(solution)/shard_map/sub | solution.py:90
  (246 shorter events, 244.4 us)
Async XLA Ops:
  6.5 126.9 %all-gather.21.cloned.1.call-start = ((), (), s32[]{:S(2)}) async-start(), calls=%async_computation.4 | async-start | bytes 10485760 | tf_op jit(solution)/shard_map/all_gather | solution.py:14
  43.1 170.1 %all-reduce.20.cloned.1.call-start = ((), (), s32[]{:S(2)}) async-start(), calls=%async_computation.15 | async-start | bytes 1048576 | tf_op jit(solution)/shard_map/psum | solution.py:75
  153.1 2.6 copy-start.2
  156.5 289.1 %all-gather.23.cloned.1.call-start = ((), (), s32[]{:S(2)}) async-start(), calls=%async_computation.5 | async-start | bytes 18874368 | tf_op jit(solution)/shard_map/all_gather | solution.py:14
  275.8 3.7 copy-start.8
  295.2 301.1 %all-gather.25.cloned.1.call-start = ((), (), s32[]{:S(2)}) async-start(), calls=%async_computation.6 | async-start | bytes 18874368 | tf_op jit(solution)/shard_map/all_gather | solution.py:14
  295.8 458.9 %all-reduce.10.cloned.1.call-start = ((), (), s32[]{:S(2)}) async-start(), calls=%async_computation | async-start | bytes 4194304 | tf_op jit(solution)/shard_map/psum | solution.py:84
  626.2 2.0 copy-start
  686.7 131.1 %all-reduce.12.cloned.1.call-start = ((), (), s32[]{:S(2)}) async-start(), calls=%async_computation.1 | async-start | bytes 524288 | tf_op jit(solution)/shard_map/psum | solution.py:86
  758.3 1.4 copy-start.5
  762.2 213.8 %all-gather.27.cloned.1.call-start = ((), (), s32[]{:S(2)}) async-start(), calls=%async_computation.7 | async-start | bytes 18874368 | tf_op jit(solution)/shard_map/all_gather | solution.py:14
  825.8 301.2 %all-gather.29.cloned.1.call-start = ((), (), s32[]{:S(2)}) async-start(), calls=%async_computation.8 | async-start | bytes 18874368 | tf_op jit(solution)/shard_map/all_gather | solution.py:14
  826.5 482.8 %all-gather.31.cloned.1.call-start = ((), (), s32[]{:S(2)}) async-start(), calls=%async_computation.9 | async-start | bytes 10485760 | tf_op jit(solution)/shard_map/all_gather | solution.py:14
  1150.2 1.6 copy-start.6
  1223.5 166.0 %all-reduce.18.cloned.1.call-start = ((), (), s32[]{:S(2)}) async-start(), calls=%async_computation.14 | async-start | bytes 1048576 | tf_op jit(solution)/shard_map/psum | solution.py:75
  1329.4 2.6 copy-start.3
  1332.8 289.6 %all-gather.33.cloned.1.call-start = ((), (), s32[]{:S(2)}) async-start(), calls=%async_computation.10 | async-start | bytes 18874368 | tf_op jit(solution)/shard_map/all_gather | solution.py:14
  1452.9 3.7 copy-start.9
  1472.0 301.1 %all-gather.35.cloned.1.call-start = ((), (), s32[]{:S(2)}) async-start(), calls=%async_computation.11 | async-start | bytes 18874368 | tf_op jit(solution)/shard_map/all_gather | solution.py:14
  1472.6 457.5 %all-reduce.14.cloned.1.call-start = ((), (), s32[]{:S(2)}) async-start(), calls=%async_computation.2 | async-start | bytes 4194304 | tf_op jit(solution)/shard_map/psum | solution.py:84
  1803.0 2.0 copy-start.1
  1862.2 131.0 %all-reduce.16.cloned.1.call-start = ((), (), s32[]{:S(2)}) async-start(), calls=%async_computation.3 | async-start | bytes 524288 | tf_op jit(solution)/shard_map/psum | solution.py:86
  1933.7 1.3 copy-start.4
  1937.6 213.8 %all-gather.39.cloned.1.call-start = ((), (), s32[]{:S(2)}) async-start(), calls=%async_computation.13 | async-start | bytes 18874368 | tf_op jit(solution)/shard_map/all_gather | solution.py:14
  2001.2 301.0 %all-gather.37.cloned.1.call-start = ((), (), s32[]{:S(2)}) async-start(), calls=%async_computation.12 | async-start | bytes 18874368 | tf_op jit(solution)/shard_map/all_gather | solution.py:14
  2325.3 1.6 copy-start.7
Sparse Core Ops, SparseCore 0:
  43.2 90.1 all-gather.20
  156.6 56.5 all-reduce.19
  295.3 150.1 all-gather.22
  447.0 149.2 all-gather.24
  686.8 67.7 all-reduce.9
  762.4 55.4 all-reduce.11
  825.9 150.1 all-gather.26
  977.7 149.2 all-gather.28
  1223.7 85.6 all-gather.30
  1332.9 56.6 all-reduce.17
  1472.2 150.1 all-gather.32
  1623.9 149.2 all-gather.34
  1862.3 67.7 all-reduce.13
  1937.8 55.4 all-reduce.15
  2001.3 150.1 all-gather.38
  2152.9 149.2 all-gather.36
